TPU v7x, 32 devices: a whole 2x2x4 slice. The times are simulated.
32 devices in a mesh: band: 4 (over x, core), tr: 4 (over z), tc: 2 (over y).
Axes of the slice: x: 2, y: 2, z: 4, core: 2. Of those that a mesh axis runs over, the one named last changes fastest.
Arguments:
- voltages: bfloat16 [4096, 2, 1024], P(('band', 'tr', 'tc')), parts along dimension 0, may hold values from -4 to 4
Outputs:
- visibilities: bfloat16 [128, 2, 1024, 1024], P(('band', 'tc'), None, 'tr'), parts along dimension 0
There are 4 independent parts, one for each index of `band`. A program takes and returns all parts, laid end to end along the dimension named above; each array names one. Nothing has to cross between parts.
All inputs are finite; a program needn't handle non-finite values.
Results may differ from a plain program's by a relative error of at most 0.0054.
Values may be sent and summed in bfloat16 or wider, within the bound.
No kernel may reach another device: no remote copies, remote signals or barrier semaphores. Data moves between devices by JAX's collectives and lax.ppermute only.
A program may use at most 64 MiB of HBM per device.

v0:
```python
import math
import jax
import jax.numpy as jnp
from jax import lax
from jax.sharding import PartitionSpec as P

FINE = 32
TAPS = 16


def shifted(block, axis, distance):
    devices = range(lax.axis_size(axis))
    route = [(i - distance, i) for i in devices if i - distance in devices]
    return lax.ppermute(block, axis, route)


def filter_taps(tap_total, fine_total):
    length = tap_total * fine_total
    position = jnp.arange(length).astype(jnp.float32)
    offset = (position - (length - 1) / 2.0) / fine_total
    prototype = jnp.sin(math.pi * offset) / (math.pi * offset)
    prototype = prototype / jnp.sqrt(jnp.sum(prototype * prototype))
    return prototype.reshape(tap_total, fine_total)


def fourier_table(fine_total):
    indices = jnp.arange(fine_total).astype(jnp.float32)
    angles = 2.0 * math.pi * jnp.mod(indices[:, None] * indices[None, :], fine_total) / fine_total
    cosine = jnp.cos(angles)
    sine_part = jnp.sin(angles)
    stacked = jnp.stack(
        [jnp.stack([cosine, -sine_part], axis=-1), jnp.stack([sine_part, cosine], axis=-1)], axis=1
    )
    return stacked.reshape(2 * fine_total, 2 * fine_total)


def filterbank(extended, hop_count):
    inputs = extended.shape[3]
    tap_table = filter_taps(TAPS, FINE)
    fourier = fourier_table(FINE)
    weighted = jnp.zeros((hop_count, FINE, 2, inputs), jnp.float32)
    for tap_index in range(TAPS):
        weighted = weighted + tap_table[tap_index][None, :, None, None] * extended[
            tap_index : tap_index + hop_count
        ].astype(jnp.float32)
    spectra = jnp.einsum(
        "sjm,jo->som",
        weighted.reshape(hop_count, 2 * FINE, inputs),
        fourier,
        precision=lax.Precision.HIGHEST,
    )
    return spectra.reshape(hop_count, FINE, 2, inputs).astype(jnp.bfloat16)


def per_device(voltages):
    samples = voltages.shape[0]
    inputs = voltages.shape[2]
    hop_count = samples // FINE
    needed = TAPS - 1
    shift_count = (needed + hop_count - 1) // hop_count
    earlier = []
    for distance in range(1, shift_count + 1):
        take_hops = min(hop_count, needed - (distance - 1) * hop_count)
        portion = voltages[samples - take_hops * FINE :]
        arrived = shifted(portion, ("tr", "tc"), distance)
        earlier = [arrived] + earlier
    extended = jnp.concatenate(earlier + [voltages], axis=0).reshape(
        needed + hop_count, FINE, 2, inputs
    )
    spectra = filterbank(extended, hop_count)
    turned = lax.all_to_all(
        lax.all_to_all(spectra, "tr", split_axis=3, concat_axis=0, tiled=True),
        "tc",
        split_axis=1,
        concat_axis=0,
        tiled=True,
    )
    spectra_total = turned.shape[0]
    swapped = jnp.stack([turned[:, :, 1], -turned[:, :, 0]], axis=2)
    stacked = jnp.stack([turned, swapped], axis=0)
    inverse_total = 1.0 / float(spectra_total)
    product = jnp.einsum(
        "rskci,skcj->krij",
        stacked,
        lax.all_gather(turned, "tr", axis=3, tiled=True),
        preferred_element_type=jnp.float32,
    )
    summed = product * inverse_total
    return summed.astype(jnp.bfloat16)


def solution(mesh):
    in_specs = (P(("band", "tr", "tc"), None, None),)
    out_specs = P(("band", "tc"), None, "tr", None)
    return jax.shard_map(
        per_device, mesh=mesh, in_specs=in_specs, out_specs=out_specs, check_vma=False
    )
```

profile of v0, /device:TPU:0, one launch (start us, length us, event | category | flops | bytes accessed | tf_op | source)
XLA Modules:
  0.0 185.9 jit_solution(17419271201619337630)
XLA Ops:
  6.5 4.9 %collective-permute-start.3 = (bf16[128,2,1024]{2,1,0:T(2,128)(2,1)}, bf16[128,2,1024]{2,1,0:T(2,128)(2,1)S(1)}, u32[]{:S(2)}, u32[]{:S(2)}) collective-permute-start(bf16[128,2,1024]{2,1,0:T(2,128)(2,1)} %param.1), channel_id=1, source_target_pairs={{0,1},{1,2},{2,3},{3,4},{4,5},{5,6},{6,7},{8,9},{9,10},{10,11},{11... | collective-permute-start | bytes 1572872 | tf_op jit(solution)/shard_map/ppermute | solution.py:14
  11.5 3.5 %collective-permute-start.2 = (bf16[128,2,1024]{2,1,0:T(2,128)(2,1)}, bf16[128,2,1024]{2,1,0:T(2,128)(2,1)S(1)}, u32[]{:S(2)}, u32[]{:S(2)}) collective-permute-start(bf16[128,2,1024]{2,1,0:T(2,128)(2,1)} %param.1), channel_id=1, source_target_pairs={{0,2},{1,3},{2,4},{3,5},{4,6},{5,7},{8,10},{9,11},{10,12},{11,13},... | collective-permute-start | bytes 1572872 | tf_op jit(solution)/shard_map/ppermute | solution.py:14
  15.0 4.4 %collective-permute-start.1 = (bf16[128,2,1024]{2,1,0:T(2,128)(2,1)}, bf16[128,2,1024]{2,1,0:T(2,128)(2,1)S(1)}, u32[]{:S(2)}, u32[]{:S(2)}) collective-permute-start(bf16[128,2,1024]{2,1,0:T(2,128)(2,1)} %param.1), channel_id=1, source_target_pairs={{0,3},{1,4},{2,5},{3,6},{4,7},{8,11},{9,12},{10,13},{11,14},{12,15... | collective-permute-start | bytes 1572872 | tf_op jit(solution)/shard_map/ppermute | solution.py:14
  19.4 1.3 slice.142
  20.7 2.0 %collective-permute-start = (bf16[96,2,1024]{2,1,0:T(2,128)(2,1)S(1)}, bf16[96,2,1024]{2,1,0:T(2,128)(2,1)S(1)}, u32[]{:S(2)}, u32[]{:S(2)}) collective-permute-start(bf16[96,2,1024]{2,1,0:T(2,128)(2,1)S(1)} %slice.142), channel_id=1, source_target_pairs={{0,4},{1,5},{2,6},{3,7},{8,12},{9,13},{10,14},{11,15},{16,20},{17,... | collective-permute-start | bytes 1179656 | tf_op jit(solution)/shard_map/ppermute | solution.py:14
  22.7 0.6 multiply_reduce_fusion
  26.2 0.6 reshape.353
  26.9 18.9 %collective-permute-done = bf16[96,2,1024]{2,1,0:T(2,128)(2,1)S(1)} collective-permute-done((bf16[96,2,1024]{2,1,0:T(2,128)(2,1)S(1)}, bf16[96,2,1024]{2,1,0:T(2,128)(2,1)S(1)}, u32[]{:S(2)}, u32[]{:S(2)}) %collective-permute-start) | collective-permute-done | bytes 393248 | tf_op jit(solution)/shard_map/ppermute | solution.py:14
  46.0 0.6 constant_dynamic-update-slice_fusion
  46.6 0.6 constant_dynamic-update-slice_fusion.2
  47.3 0.6 constant_dynamic-update-slice_fusion.4
  48.3 7.2 %multiply_add_fusion = f32[128,2,1024]{2,1,0:T(2,128)S(1)} fusion(bf16[128,2,1024]{2,1,0:T(2,128)(2,1)S(1)} %copy-done.1, bf16[128,2,1024]{2,1,0:T(2,128)(2,1)S(1)} %collective-permute-done.3, bf16[128,2,1024]{2,1,0:T(2,128)(2,1)S(1)} %collective-permute-done.2, bf16[128,2,1024]{2,1,0:T(2,128)(2,1)S(1)} %collective-permute-done.1, f32[128]{0:T(128)S(1)} %mul.356, ...), kind=kLoop, calls=%fused_computation.7 | loop fusion | flops 12320768 | bytes 9445376 | tf_op jit(solution)/shard_map/add | solution.py:43
  55.5 0.7 add.121
  56.2 1.0 fusion.2
  57.5 1.9 %copy.18 = bf16[4,32,2,1024]{1,2,0,3:T(2,128)(2,1)S(1)} copy(bf16[4,32,2,1024]{3,2,1,0:T(2,128)(2,1)S(1)} %convert_element_type.138) | data formatting | bytes 1048576 | tf_op jit(solution)/shard_map/convert_element_type | solution.py:52
  59.4 2.2 %reshape.354 = bf16[4,2,32768]{2,1,0:T(2,128)(2,1)S(1)} reshape(bf16[1024,4,2,32]{3,2,1,0:T(2,128)(2,1)S(1)} %bitcast.32) | data formatting | bytes 1048576
  61.6 39.0 %all_to_all.36 = bf16[4,2,32768]{2,1,0:T(2,128)(2,1)S(1)} all-to-all(bf16[4,2,32768]{2,1,0:T(2,128)(2,1)S(1)} %reshape.354), channel_id=1, replica_groups=mesh['band'=4,'tr'=4,'tc'=2] {'tr'}, dimensions={0} | all-to-all | bytes 1048576 | tf_op jit(solution)/shard_map/all_to_all | solution.py:72
  100.6 1.1 reshape.355
  101.6 2.8 %copy.30 = bf16[4,32,2,4,256]{4,3,1,2,0:T(4,128)(2,1)S(1)} copy(bf16[4,32,2,4,256]{1,2,0,4,3:T(2,128)(2,1)S(1)} %bitcast.33) | data formatting | bytes 1048576 | tf_op jit(solution)/shard_map/all_to_all | solution.py:72
  105.1 17.1 %all_to_all.37 = bf16[16,32,2,256]{3,2,0,1:T(2,128)(2,1)S(1)} all-to-all(bf16[16,32,2,256]{3,2,0,1:T(2,128)(2,1)S(1)} %copy.21), channel_id=1, replica_groups=mesh['band'=4,'tr'=4,'tc'=2] {'tc'}, dimensions={1} | all-to-all | bytes 1048576 | tf_op jit(solution)/shard_map/all_to_all | solution.py:71
  122.5 1.1 copy.23
  123.7 1.1 fusion.13
  124.8 44.1 %all-gather.2.cloned.1.call-done = bf16[32,16,2,1024]{3,0,2,1:T(8,128)(2,1)} async-done(((bf16[32,16,2,256]{3,0,2,1:T(8,128)(2,1)}), bf16[32,16,2,1024]{3,0,2,1:T(8,128)(2,1)}) %all-gather.2.cloned.1.call-update) | async-done | bytes 2097168 | tf_op jit(solution)/shard_map/all_gather | solution.py:85
  168.9 10.1 %fusion = bf16[16,2,256,1024]{3,2,1,0:T(8,128)(2,1)} fusion(bf16[32,16,2,1024]{3,0,2,1:T(8,128)(2,1)} %all-gather.2.cloned.1.call-done, bf16[1,32,16,2,256]{4,1,3,2,0:T(8,128)(2,1)S(1)} %maximum_bitcast_fusion, bf16[1,32,16,2,256]{4,1,3,2,0:T(8,128)(2,1)S(1)} %bitcast.36), kind=kOutput, calls=%fused_computation.1 | convolution fusion | flops 1091043328 | bytes 19922944 | tf_op jit(solution)/shard_map/rskci,skcj->krij/dot_general | solution.py:82
  (55 shorter events, 4.0 us)
Async XLA Ops:
  6.5 162.4 %all-gather.2.cloned.1.call-start = ((), (), s32[]{:S(2)}) async-start(), calls=%async_computation.2 | async-start | bytes 2621440 | tf_op jit(solution)/shard_map/all_gather | solution.py:85
  6.5 40.7 %collective-permute-start.3 = (bf16[128,2,1024]{2,1,0:T(2,128)(2,1)}, bf16[128,2,1024]{2,1,0:T(2,128)(2,1)S(1)}, u32[]{:S(2)}, u32[]{:S(2)}) collective-permute-start(bf16[128,2,1024]{2,1,0:T(2,128)(2,1)} %param.1), channel_id=1, source_target_pairs={{0,1},{1,2},{2,3},{3,4},{4,5},{5,6},{6,7},{8,9},{9,10},{10,11},{11... | collective-permute-start | bytes 1572872 | tf_op jit(solution)/shard_map/ppermute | solution.py:14
  11.5 35.2 %collective-permute-start.2 = (bf16[128,2,1024]{2,1,0:T(2,128)(2,1)}, bf16[128,2,1024]{2,1,0:T(2,128)(2,1)S(1)}, u32[]{:S(2)}, u32[]{:S(2)}) collective-permute-start(bf16[128,2,1024]{2,1,0:T(2,128)(2,1)} %param.1), channel_id=1, source_target_pairs={{0,2},{1,3},{2,4},{3,5},{4,6},{5,7},{8,10},{9,11},{10,12},{11,13},... | collective-permute-start | bytes 1572872 | tf_op jit(solution)/shard_map/ppermute | solution.py:14
  15.0 31.1 %collective-permute-start.1 = (bf16[128,2,1024]{2,1,0:T(2,128)(2,1)}, bf16[128,2,1024]{2,1,0:T(2,128)(2,1)S(1)}, u32[]{:S(2)}, u32[]{:S(2)}) collective-permute-start(bf16[128,2,1024]{2,1,0:T(2,128)(2,1)} %param.1), channel_id=1, source_target_pairs={{0,3},{1,4},{2,5},{3,6},{4,7},{8,11},{9,12},{10,13},{11,14},{12,15... | collective-permute-start | bytes 1572872 | tf_op jit(solution)/shard_map/ppermute | solution.py:14
  20.7 25.0 %collective-permute-start = (bf16[96,2,1024]{2,1,0:T(2,128)(2,1)S(1)}, bf16[96,2,1024]{2,1,0:T(2,128)(2,1)S(1)}, u32[]{:S(2)}, u32[]{:S(2)}) collective-permute-start(bf16[96,2,1024]{2,1,0:T(2,128)(2,1)S(1)} %slice.142), channel_id=1, source_target_pairs={{0,4},{1,5},{2,6},{3,7},{8,12},{9,13},{10,14},{11,15},{16,20},{17,... | collective-permute-start | bytes 1179656 | tf_op jit(solution)/shard_map/ppermute | solution.py:14
  46.0 1.9 copy-start.1
  123.6 45.3 %copy-start = (bf16[2,16,16,2,256]{4,1,0,3,2:T(8,128)(2,1)S(1)}, bf16[2,16,16,2,256]{4,1,0,3,2:T(8,128)(2,1)}, u32[]{:S(2)}) copy-start(bf16[2,16,16,2,256]{4,1,0,3,2:T(8,128)(2,1)} %copy.23) | copy-start | bytes 1572868
Sparse Core Ops, SparseCore 0:
  123.8 45.1 all-gather.1
where the time goes:
time: 186 us
  waiting for transfers between devices  63 us (34%)
  blocking collectives  56.1 us (30%)
  local copies, waits for them, and re-layouts  17.3 us (9%)
  starting transfers between devices  14.8 us (8%)
  between operations  14.3 us (8%)
  matrix products  11.2 us (6%)
  other arithmetic  9.29 us (5%)
    all_gather x1, waiting for transfers between devices, per_device(): lax.all_gather(turned, 'tr', axis=3, tiled=True)  44.1 us
    all_to_all x1, blocking collectives, per_device(): lax.all_to_all(spectra, 'tr', split_axis=3, concat_axis=0, tiled=True)  39 us
    ppermute x4, waiting for transfers between devices, shifted(): return lax.ppermute(block, axis, route)  18.9 us
    all_to_all x1, blocking collectives, per_device(): lax.all_to_all(lax.all_to_all(spectra, 'tr', split_axis=3, concat_axis=0,...  17.1 us
    ppermute x4, starting transfers between devices, shifted(): return lax.ppermute(block, axis, route)  14.8 us
    dot_general x1, matrix products, per_device(): jnp.einsum('rskci,skcj->krij', stacked, lax.all_gather(turned, 'tr', axis...  10.1 us
    add x1, other arithmetic, filterbank(): weighted + tap_table[tap_index][None, :, None, None] * extended[tap_index...  7.23 us
  transfers between devices with their start and end apart: 5, of which 2 were waited for; matrix products, arithmetic and copies ran while one was open for 4% of the time, Pallas kernels for 0%

commit v1 on v0

--- a/solution.py
+++ b/solution.py
@@ -53,6 +53,41 @@
 
 
 def per_device(voltages):
+
+    def deliver_area_up(z_in, u):
+        comm_axis = "tr"
+        part_next = lax.axis_size(comm_axis)
+        small = lax.axis_index(comm_axis)
+        y, tile_out, next_value = (part_next, small, z_in.shape[3])
+        state_now = range(y)
+        prior = map(lambda dev_j: (dev_j, (dev_j + 1) % y), state_now)
+        bank = list(prior)
+        steps_seen = [(it, i0) for i0, it in bank]
+        part_now = lax.ppermute(z_in, comm_axis, bank)
+        val2 = lax.ppermute(z_in, axis_name=comm_axis, perm=steps_seen)
+        carry_out, y1 = (part_now, val2)
+        u_next = u(z_in, tile_out * next_value)
+        top = u_next.shape[3]
+        f_now = jnp.zeros((*u_next.shape[:3], y * top, *u_next.shape[4:]), u_next.dtype)
+
+        def attach_meshes_here(f_now, u_next, fresh):
+            return lax.dynamic_update_slice_in_dim(f_now, u_next, fresh * top, axis=3)
+
+        f_now = attach_meshes_here(f_now, u_next, tile_out)
+        for k0 in [*range(1, y // 2 + 1)]:
+            e_now, oldest = ((tile_out - k0) % y, (tile_out + k0) % y)
+            current_value = (carry_out, y1)
+            if k0 < y // 2:
+                built = lax.ppermute(carry_out, axis_name=comm_axis, perm=bank)
+                reply = lax.ppermute(y1, comm_axis, perm=steps_seen)
+                carry_out, y1 = (built, reply)
+            piece_next = u(current_value[0], e_now * next_value)
+            f_now = attach_meshes_here(f_now, piece_next, e_now)
+            if 2 * k0 < y:
+                all_values = u(current_value[1], oldest * next_value)
+                f_now = attach_meshes_here(f_now, all_values, oldest)
+        return f_now
+
     samples = voltages.shape[0]
     inputs = voltages.shape[2]
     hop_count = samples // FINE
@@ -79,11 +114,11 @@
     swapped = jnp.stack([turned[:, :, 1], -turned[:, :, 0]], axis=2)
     stacked = jnp.stack([turned, swapped], axis=0)
     inverse_total = 1.0 / float(spectra_total)
-    product = jnp.einsum(
-        "rskci,skcj->krij",
-        stacked,
-        lax.all_gather(turned, "tr", axis=3, tiled=True),
-        preferred_element_type=jnp.float32,
+    product = deliver_area_up(
+        turned,
+        lambda part, offset_2: jnp.einsum(
+            "rskci,skcj->krij", stacked, part, preferred_element_type=jnp.float32
+        ),
     )
     summed = product * inverse_total
     return summed.astype(jnp.bfloat16)

time: 186 us -> 171 us (0.919)
  waiting for transfers between devices: 63 us -> 45.9 us
  starting transfers between devices: 14.8 us -> 30.8 us
  blocking collectives: 56.1 us -> 41 us
  between operations: 14.3 us -> 0.95 us
  other arithmetic: 9.29 us -> 17.5 us
  local copies, waits for them, and re-layouts: 17.3 us -> 22.5 us
    all_gather x1 -> x0, waiting for transfers between devices: 44.1 us -> none  [per_device(): lax.all_gather(turned, 'tr', axis=3, tiled=True)]
    ppermute x0 -> x3, waiting for transfers between devices: none -> 20.7 us  [the longest x1 9.41 us: deliver_area_up(): built = lax.ppermute(carry_out, axis_name=comm_axis, perm=bank)]
    all_to_all x1 -> x0, blocking collectives: 17.1 us -> none  [per_device(): lax.all_to_all(lax.all_to_all(spectra, 'tr', split_axis=3, concat_axis=0,...]
    all_to_all x0 -> x1, starting transfers between devices: none -> 12.7 us  [per_device(): lax.all_to_all(lax.all_to_all(spectra, 'tr', split_axis=3, concat_axis=0,...]
    convert_element_type x0 -> x1, other arithmetic: none -> 8.37 us  [per_device(): return summed.astype(jnp.bfloat16)]
    all_to_all x0 -> x1, waiting for transfers between devices: none -> 8.01 us  [per_device(): lax.all_to_all(lax.all_to_all(spectra, 'tr', split_axis=3, concat_axis=0,...]
    broadcast_in_dim x0 -> x1, local copies, waits for them, and re-layouts: none -> 4.2 us  [deliver_area_up(): jnp.zeros((*u_next.shape[:3], y * top, *u_next.shape[4:]), u_next.dtype)]
    ppermute x0 -> x3, starting transfers between devices: none -> 3.87 us  [the longest x1 3.81 us: deliver_area_up(): val2 = lax.ppermute(z_in, axis_name=comm_axis, perm=steps_seen)]
  transfers between devices with their start and end apart: 5 -> 8, of which waited for: 2 -> 5; matrix products, arithmetic and copies ran while one was open for 4% -> 11% of each run, Pallas kernels for 0% -> 0%
where the time goes in v1:
time: 171 us; the launch traced here: 170 us
  waiting for transfers between devices  45.9 us (27%)
  blocking collectives  41 us (24%)
  starting transfers between devices  30.8 us (18%)
  local copies, waits for them, and re-layouts  22.5 us (13%)
  other arithmetic  17.5 us (10%)
  matrix products  11.6 us (7%)
    all_to_all x1, blocking collectives, per_device(): lax.all_to_all(spectra, 'tr', split_axis=3, concat_axis=0, tiled=True)  41 us
    ppermute x4, waiting for transfers between devices, shifted(): return lax.ppermute(block, axis, route)  17.3 us
    ppermute x4, starting transfers between devices, shifted(): return lax.ppermute(block, axis, route)  14.3 us
    all_to_all x1, starting transfers between devices, per_device(): lax.all_to_all(lax.all_to_all(spectra, 'tr', split_axis=3, concat_axis=0,...  12.7 us
    dot_general x4, matrix products, per_device(): jnp.einsum('rskci,skcj->krij', stacked, part, preferred_element_type=jnp....  10.5 us
    ppermute x1, waiting for transfers between devices, deliver_area_up(): built = lax.ppermute(carry_out, axis_name=comm_axis, perm=bank)  9.41 us
    convert_element_type x1, other arithmetic, per_device(): return summed.astype(jnp.bfloat16)  8.37 us
    add x1, other arithmetic, filterbank(): weighted + tap_table[tap_index][None, :, None, None] * extended[tap_index...  8.17 us
  transfers between devices with their start and end apart: 8, of which 5 were waited for; matrix products, arithmetic and copies ran while one was open for 11% of the time, Pallas kernels for 0%

profile of v1, /device:TPU:0, one launch (start us, length us, event | category | flops | bytes accessed | tf_op | source)
XLA Modules:
  0.0 170.2 jit_solution(11269883623825842210)
XLA Ops:
  0.0 5.9 %collective-permute-start.1 = (bf16[128,2,1024]{2,1,0:T(2,128)(2,1)}, bf16[128,2,1024]{2,1,0:T(2,128)(2,1)S(1)}, u32[]{:S(2)}, u32[]{:S(2)}) collective-permute-start(bf16[128,2,1024]{2,1,0:T(2,128)(2,1)} %param.1), channel_id=1, source_target_pairs={{0,3},{1,4},{2,5},{3,6},{4,7},{8,11},{9,12},{10,13},{11,14},{12,15... | collective-permute-start | bytes 1572872 | tf_op jit(solution)/shard_map/ppermute | solution.py:14
  5.9 3.5 %collective-permute-start.2 = (bf16[128,2,1024]{2,1,0:T(2,128)(2,1)}, bf16[128,2,1024]{2,1,0:T(2,128)(2,1)S(1)}, u32[]{:S(2)}, u32[]{:S(2)}) collective-permute-start(bf16[128,2,1024]{2,1,0:T(2,128)(2,1)} %param.1), channel_id=1, source_target_pairs={{0,2},{1,3},{2,4},{3,5},{4,6},{5,7},{8,10},{9,11},{10,12},{11,13},... | collective-permute-start | bytes 1572872 | tf_op jit(solution)/shard_map/ppermute | solution.py:14
  9.5 3.4 %collective-permute-start.3 = (bf16[128,2,1024]{2,1,0:T(2,128)(2,1)}, bf16[128,2,1024]{2,1,0:T(2,128)(2,1)S(1)}, u32[]{:S(2)}, u32[]{:S(2)}) collective-permute-start(bf16[128,2,1024]{2,1,0:T(2,128)(2,1)} %param.1), channel_id=1, source_target_pairs={{0,1},{1,2},{2,3},{3,4},{4,5},{5,6},{6,7},{8,9},{9,10},{10,11},{11... | collective-permute-start | bytes 1572872 | tf_op jit(solution)/shard_map/ppermute | solution.py:14
  14.2 1.4 collective-permute-start
  19.8 17.3 %collective-permute-done = bf16[96,2,1024]{2,1,0:T(2,128)(2,1)S(1)} collective-permute-done((bf16[96,2,1024]{2,1,0:T(2,128)(2,1)S(1)}, bf16[96,2,1024]{2,1,0:T(2,128)(2,1)S(1)}, u32[]{:S(2)}, u32[]{:S(2)}) %collective-permute-start) | collective-permute-done | bytes 393248 | tf_op jit(solution)/shard_map/ppermute | solution.py:14
  39.2 1.4 constant_dynamic-update-slice_fusion.6
  40.6 8.2 %multiply_add_fusion = f32[128,2,1024]{2,1,0:T(2,128)S(1)} fusion(bf16[128,2,1024]{2,1,0:T(2,128)(2,1)} %param.1, bf16[128,2,1024]{2,1,0:T(2,128)(2,1)S(1)} %collective-permute-done.3, bf16[128,2,1024]{2,1,0:T(2,128)(2,1)S(1)} %collective-permute-done.2, bf16[128,2,1024]{2,1,0:T(2,128)(2,1)S(1)} %collective-permute-done.1, f32[128]{0:T(128)S(1)} %mul.368, ...), kind=kLoop, calls=%fused_computation.8 | loop fusion | flops 12320768 | bytes 9445376 | tf_op jit(solution)/shard_map/add | solution.py:43
  50.7 1.9 %copy.27 = bf16[4,32,2,1024]{1,2,0,3:T(2,128)(2,1)S(1)} copy(bf16[4,32,2,1024]{3,2,1,0:T(2,128)(2,1)S(1)} %convert_element_type.138) | data formatting | bytes 1048576 | tf_op jit(solution)/shard_map/convert_element_type | solution.py:52
  52.7 2.2 %reshape.360 = bf16[4,2,32768]{2,1,0:T(2,128)(2,1)S(1)} reshape(bf16[1024,4,2,32]{3,2,1,0:T(2,128)(2,1)S(1)} %bitcast.62) | data formatting | bytes 1048576
  54.8 41.0 %all_to_all.36 = bf16[4,2,32768]{2,1,0:T(2,128)(2,1)S(1)} all-to-all(bf16[4,2,32768]{2,1,0:T(2,128)(2,1)S(1)} %reshape.360), channel_id=1, replica_groups=mesh['band'=4,'tr'=4,'tc'=2] {'tr'}, dimensions={0} | all-to-all | bytes 1048576 | tf_op jit(solution)/shard_map/all_to_all | solution.py:107
  96.9 2.8 %copy.48 = bf16[4,32,2,4,256]{4,3,1,2,0:T(4,128)(2,1)S(1)} copy(bf16[4,32,2,4,256]{1,2,0,4,3:T(2,128)(2,1)S(1)} %bitcast.63) | data formatting | bytes 1048576 | tf_op jit(solution)/shard_map/all_to_all | solution.py:107
  99.8 1.3 copy.30
  101.2 12.7 %all-to-all-start.1 = ((bf16[16,32,2,256]{3,2,0,1:T(2,128)(2,1)}), bf16[16,32,2,256]{3,2,0,1:T(2,128)(2,1)S(1)}, u32[]{:S(2)}, u32[]{:S(2)}) async-start(bf16[16,32,2,256]{3,2,0,1:T(2,128)(2,1)} %copy.30), calls=%async_computation.1 | async-start | bytes 1048576 | tf_op jit(solution)/shard_map/all_to_all | solution.py:106
  113.8 8.0 %all-to-all-done.1 = bf16[16,32,2,256]{3,2,0,1:T(2,128)(2,1)S(1)} async-done(((bf16[16,32,2,256]{3,2,0,1:T(2,128)(2,1)}), bf16[16,32,2,256]{3,2,0,1:T(2,128)(2,1)S(1)}, u32[]{:S(2)}, u32[]{:S(2)}) %all-to-all-start.1) | async-done | bytes 524320 | tf_op jit(solution)/shard_map/all_to_all | solution.py:106
  122.6 3.8 %collective-permute-start.5 = (bf16[32,16,2,256]{3,0,2,1:T(8,128)(2,1)S(1)}, bf16[32,16,2,256]{3,0,2,1:T(8,128)(2,1)S(1)}, u32[]{:S(2)}, u32[]{:S(2)}) collective-permute-start(bf16[32,16,2,256]{3,0,2,1:T(8,128)(2,1)S(1)} %bitcast.56), channel_id=1, source_target_pairs={{2,0},{4,2},{6,4},{0,6},{3,1},{5,3},{7,5},{1,7},{10,8},{12,10},{14... | collective-permute-start | bytes 1572872 | tf_op jit(solution)/shard_map/ppermute | solution.py:67
  126.4 4.2 %broadcast_in_dim.2 = f32[16,2,256,1024]{3,2,1,0:T(8,128)S(1)} broadcast(f32[]{:T(128)} %constant.49.clone.1), dimensions={} | broadcast | bytes 33554436 | tf_op jit(solution)/shard_map/broadcast_in_dim | solution.py:71
  130.6 2.6 %bitcast_dynamic-update-slice_fusion.3 = f32[16,2,256,1024]{3,2,1,0:T(8,128)S(1)} fusion(f32[16,2,256,1024]{3,2,1,0:T(8,128)S(1)} %broadcast_in_dim.2, s32[]{:T(128)S(6)} %select_n.53, bf16[32,16,2,256,1]{3,0,2,4,1:T(8,128)(2,1)S(1)} %bitcast.57, bf16[1,32,16,2,256]{4,1,3,2,0:T(8,128)(2,1)S(1)} %maximum_bitcast_fusion, ...), kind=kOutput, calls=%fused_computation.4 | convolution fusion | flops 268959744 | bytes 9961476 | tf_op jit(solution)/shard_map/rskci,skcj->krij/dot_general | solution.py:119
  133.3 5.9 %collective-permute-done.4 = bf16[32,16,2,256]{3,0,2,1:T(8,128)(2,1)S(1)} collective-permute-done((bf16[32,16,2,256]{3,0,2,1:T(8,128)(2,1)S(1)}, bf16[32,16,2,256]{3,0,2,1:T(8,128)(2,1)S(1)}, u32[]{:S(2)}, u32[]{:S(2)}) %collective-permute-start.4) | collective-permute-done | bytes 524320 | tf_op jit(solution)/shard_map/ppermute | solution.py:66
  139.1 2.6 %bitcast_dynamic-update-slice_fusion.2 = f32[16,2,256,1024]{3,2,1,0:T(8,128)S(1)} fusion(f32[16,2,256,1024]{3,2,1,0:T(8,128)S(1)} %bitcast_dynamic-update-slice_fusion.3, s32[]{:T(128)S(6)} %select_n.55, bf16[32,16,2,256]{3,0,2,1:T(8,128)(2,1)S(1)} %collective-permute-done.4, bf16[1,32,16,2,256]{4,1,3,2,0:T(8,128)(2,1)S(1)} %maximum_bitcast_fusion, ...), kind=kOutput, calls=%fused_computation.3 | convolution fusion | flops 268959744 | bytes 9961476 | tf_op jit(solution)/shard_map/rskci,skcj->krij/dot_general | solution.py:119
  141.8 5.4 %collective-permute-done.5 = bf16[32,16,2,256]{3,0,2,1:T(8,128)(2,1)S(1)} collective-permute-done((bf16[32,16,2,256]{3,0,2,1:T(8,128)(2,1)S(1)}, bf16[32,16,2,256]{3,0,2,1:T(8,128)(2,1)S(1)}, u32[]{:S(2)}, u32[]{:S(2)}) %collective-permute-start.5) | collective-permute-done | bytes 524320 | tf_op jit(solution)/shard_map/ppermute | solution.py:67
  147.2 2.6 %bitcast_dynamic-update-slice_fusion.1 = f32[16,2,256,1024]{3,2,1,0:T(8,128)S(1)} fusion(f32[16,2,256,1024]{3,2,1,0:T(8,128)S(1)} %bitcast_dynamic-update-slice_fusion.2, s32[]{:T(128)S(6)} %select_n.57, bf16[32,16,2,256]{3,0,2,1:T(8,128)(2,1)S(1)} %collective-permute-done.5, bf16[1,32,16,2,256]{4,1,3,2,0:T(8,128)(2,1)S(1)} %maximum_bitcast_fusion, ...), kind=kOutput, calls=%fused_computation.2 | convolution fusion | flops 268959744 | bytes 9961476 | tf_op jit(solution)/shard_map/rskci,skcj->krij/dot_general | solution.py:119
  149.8 9.4 %collective-permute-done.6 = bf16[32,16,2,256]{3,0,2,1:T(8,128)(2,1)S(1)} collective-permute-done((bf16[32,16,2,256]{3,0,2,1:T(8,128)(2,1)S(1)}, bf16[32,16,2,256]{3,0,2,1:T(8,128)(2,1)S(1)}, u32[]{:S(2)}, u32[]{:S(2)}) %collective-permute-start.6) | collective-permute-done | bytes 524320 | tf_op jit(solution)/shard_map/ppermute | solution.py:81
  159.2 2.6 %bitcast_dynamic-update-slice_fusion = f32[16,2,256,1024]{3,2,1,0:T(8,128)S(1)} fusion(f32[16,2,256,1024]{3,2,1,0:T(8,128)S(1)} %bitcast_dynamic-update-slice_fusion.1, s32[]{:T(128)S(6)} %select_n.59, bf16[32,16,2,256]{3,0,2,1:T(8,128)(2,1)S(1)} %collective-permute-done.6, bf16[1,32,16,2,256]{4,1,3,2,0:T(8,128)(2,1)S(1)} %maximum_bitcast_fusion, ...), kind=kOutput, calls=%fused_computation.1 | convolution fusion | flops 268959744 | bytes 9961476 | tf_op jit(solution)/shard_map/rskci,skcj->krij/dot_general | solution.py:119
  161.9 8.4 %multiply_convert_fusion = bf16[16,2,256,1024]{3,2,1,0:T(8,128)(2,1)} fusion(f32[16,2,256,1024]{3,2,1,0:T(8,128)S(1)} %bitcast_dynamic-update-slice_fusion), kind=kLoop, calls=%fused_computation | loop fusion | flops 16777216 | bytes 50331648 | tf_op jit(solution)/shard_map/convert_element_type | solution.py:124
  (60 shorter events, 10.7 us)
Async XLA Ops:
  0.0 37.3 %collective-permute-start.1 = (bf16[128,2,1024]{2,1,0:T(2,128)(2,1)}, bf16[128,2,1024]{2,1,0:T(2,128)(2,1)S(1)}, u32[]{:S(2)}, u32[]{:S(2)}) collective-permute-start(bf16[128,2,1024]{2,1,0:T(2,128)(2,1)} %param.1), channel_id=1, source_target_pairs={{0,3},{1,4},{2,5},{3,6},{4,7},{8,11},{9,12},{10,13},{11,14},{12,15... | collective-permute-start | bytes 1572872 | tf_op jit(solution)/shard_map/ppermute | solution.py:14
  5.9 32.0 %collective-permute-start.2 = (bf16[128,2,1024]{2,1,0:T(2,128)(2,1)}, bf16[128,2,1024]{2,1,0:T(2,128)(2,1)S(1)}, u32[]{:S(2)}, u32[]{:S(2)}) collective-permute-start(bf16[128,2,1024]{2,1,0:T(2,128)(2,1)} %param.1), channel_id=1, source_target_pairs={{0,2},{1,3},{2,4},{3,5},{4,6},{5,7},{8,10},{9,11},{10,12},{11,13},... | collective-permute-start | bytes 1572872 | tf_op jit(solution)/shard_map/ppermute | solution.py:14
  9.5 29.1 %collective-permute-start.3 = (bf16[128,2,1024]{2,1,0:T(2,128)(2,1)}, bf16[128,2,1024]{2,1,0:T(2,128)(2,1)S(1)}, u32[]{:S(2)}, u32[]{:S(2)}) collective-permute-start(bf16[128,2,1024]{2,1,0:T(2,128)(2,1)} %param.1), channel_id=1, source_target_pairs={{0,1},{1,2},{2,3},{3,4},{4,5},{5,6},{6,7},{8,9},{9,10},{10,11},{11... | collective-permute-start | bytes 1572872 | tf_op jit(solution)/shard_map/ppermute | solution.py:14
  14.2 22.8 %collective-permute-start = (bf16[96,2,1024]{2,1,0:T(2,128)(2,1)S(1)}, bf16[96,2,1024]{2,1,0:T(2,128)(2,1)S(1)}, u32[]{:S(2)}, u32[]{:S(2)}) collective-permute-start(bf16[96,2,1024]{2,1,0:T(2,128)(2,1)S(1)} %slice.142), channel_id=1, source_target_pairs={{0,4},{1,5},{2,6},{3,7},{8,12},{9,13},{10,14},{11,15},{16,20},{17,... | collective-permute-start | bytes 1179656 | tf_op jit(solution)/shard_map/ppermute | solution.py:14
  101.2 20.7 %all-to-all-start.1 = ((bf16[16,32,2,256]{3,2,0,1:T(2,128)(2,1)}), bf16[16,32,2,256]{3,2,0,1:T(2,128)(2,1)S(1)}, u32[]{:S(2)}, u32[]{:S(2)}) async-start(bf16[16,32,2,256]{3,2,0,1:T(2,128)(2,1)} %copy.30), calls=%async_computation.1 | async-start | bytes 1048576 | tf_op jit(solution)/shard_map/all_to_all | solution.py:106
  122.5 16.6 %collective-permute-start.4 = (bf16[32,16,2,256]{3,0,2,1:T(8,128)(2,1)S(1)}, bf16[32,16,2,256]{3,0,2,1:T(8,128)(2,1)S(1)}, u32[]{:S(2)}, u32[]{:S(2)}) collective-permute-start(bf16[32,16,2,256]{3,0,2,1:T(8,128)(2,1)S(1)} %bitcast.55), channel_id=1, source_target_pairs={{0,2},{2,4},{4,6},{6,0},{1,3},{3,5},{5,7},{7,1},{8,10},{10,12},{12... | collective-permute-start | bytes 1572872 | tf_op jit(solution)/shard_map/ppermute | solution.py:66
  122.6 24.6 %collective-permute-start.5 = (bf16[32,16,2,256]{3,0,2,1:T(8,128)(2,1)S(1)}, bf16[32,16,2,256]{3,0,2,1:T(8,128)(2,1)S(1)}, u32[]{:S(2)}, u32[]{:S(2)}) collective-permute-start(bf16[32,16,2,256]{3,0,2,1:T(8,128)(2,1)S(1)} %bitcast.56), channel_id=1, source_target_pairs={{2,0},{4,2},{6,4},{0,6},{3,1},{5,3},{7,5},{1,7},{10,8},{12,10},{14... | collective-permute-start | bytes 1572872 | tf_op jit(solution)/shard_map/ppermute | solution.py:67
  139.1 20.1 %collective-permute-start.6 = (bf16[32,16,2,256]{3,0,2,1:T(8,128)(2,1)S(1)}, bf16[32,16,2,256]{3,0,2,1:T(8,128)(2,1)S(1)}, u32[]{:S(2)}, u32[]{:S(2)}) collective-permute-start(bf16[32,16,2,256]{3,0,2,1:T(8,128)(2,1)S(1)} %collective-permute-done.4), channel_id=1, source_target_pairs={{0,2},{2,4},{4,6},{6,0},{1,3},{3,5},{5,7},{7,1},{8,10},{10,12},{12... | collective-permute-start | bytes 1572872 | tf_op jit(solution)/shard_map/ppermute | solution.py:81
